TPU v7x, 512 devices: a whole 4x8x8 slice. The times are simulated.
512 devices in a mesh: seq: 64 (over y, x, core), expert: 8 (over z).
Axes of the slice: x: 4, y: 8, z: 8, core: 2. Of those that a mesh axis runs over, the one named last changes fastest.
Arguments:
- query_cols: bfloat16 [256, 131072], P('expert', 'seq'), may hold values from -16 to 16
- key_cols: bfloat16 [256, 131072], P('expert', 'seq'), may hold values from -6 to 6
- value_cols: bfloat16 [256, 131072], P('expert', 'seq'), may hold values from -12 to 12
- block_list: int32 [1024, 4], P('seq'), may hold values from 0 to 1023, as said below
- residual: bfloat16 [131072, 256], P(('seq', 'expert')), may hold values from -6 to 6
- out_proj: bfloat16 [256, 256], replicated, may hold values from -0.375 to 0.375
- norm_gain: float32 [256], replicated, may hold values from 0.1 to 1.9
- router_weight: bfloat16 [256, 16], replicated, may hold values from -0.375 to 0.375
- expert_ids: int32 [131072, 2], P(('seq', 'expert')), may hold values from 0 to 15, all different within a row; in each aligned block of 256 rows (0 to 255, 256 to 511, ...) at most 64 rows name the same one
- expert_in: bfloat16 [16, 256, 512], P('expert'), may hold values from -0.375 to 0.375
- expert_out: bfloat16 [16, 512, 256], P('expert'), may hold values from -0.25 to 0.25
- cotangent: bfloat16 [131072, 256], P(('seq', 'expert')), may hold values from -6 to 6
Outputs:
- layer_out: bfloat16 [131072, 256], P(('seq', 'expert'))
- grad_stream: bfloat16 [131072, 256], P(('seq', 'expert'))
- grad_w_in: float32 [16, 256, 512], P('expert')
- grad_w_out: float32 [16, 512, 256], P('expert')
Inputs may be any that keep to these rules, and one draw needn't show every extreme that they name: `block_list`: global key block ids. Among the entries of the 16 query blocks of one seq index, no owner index (id // 16) appears more than 2 times, and one owner, the same for every seq index, appears exactly 2 times. A row may repeat a block. `expert_ids`: each row names 2 different experts; in each aligned block of 256 rows (the rows of one device) no expert is named more than 64 times.
All inputs are finite; a program needn't handle non-finite values.
Results may differ from a plain program's by a relative error of at most 0.0081.
Values may be sent and summed in bfloat16 or wider, within the bound.
A program may use at most 64 MiB of HBM per device.

v0:
```python
import math

import jax
import jax.numpy as jnp
from jax import lax
from jax.sharding import PartitionSpec as P

HD = 32


norm_eps = 1e-05
root_two_pi = 0.7978845608028654
cubic_term = 0.044715


def gelu_value(preact):
    inside = root_two_pi * (preact + cubic_term * preact * preact * preact)
    return 0.5 * preact * (1.0 + jnp.tanh(inside))


def gelu_slope(preact):
    inside = root_two_pi * (preact + cubic_term * preact * preact * preact)
    tanh_value = jnp.tanh(inside)
    return 0.5 * (1.0 + tanh_value) + 0.5 * preact * (
        1.0 - tanh_value * tanh_value
    ) * root_two_pi * (1.0 + 3.0 * cubic_term * preact * preact)


def attention(query_cols, key_cols, value_cols, block_list):
    seq_count = lax.axis_size("seq")
    feat_dev, node_seq = query_cols.shape
    blk_seq, degree = block_list.shape
    block_len = node_seq // blk_seq
    heads_dev = feat_dev // HD
    pair_count = blk_seq * degree
    capacity = 2 * pair_count // seq_count
    owner_ids = (block_list // blk_seq).reshape(-1)
    local_ids = (block_list % blk_seq).reshape(-1)
    owner_hot = (owner_ids[:, None] == jnp.arange(seq_count, dtype=jnp.int32)[None, :]).astype(
        jnp.int32
    )
    slot_rank = jnp.sum((jnp.cumsum(owner_hot, 0) - owner_hot) * owner_hot, 1)
    slot_index = owner_ids * capacity + slot_rank
    wanted = jnp.zeros((seq_count * capacity,), jnp.int32).at[slot_index].set(local_ids)
    incoming = lax.all_to_all(
        wanted.reshape(seq_count, capacity), "seq", split_axis=0, concat_axis=0, tiled=True
    )
    local_pairs = jnp.concatenate([key_cols, value_cols], 0).reshape(
        2 * feat_dev, blk_seq, block_len
    )
    replies = jnp.take(local_pairs, incoming.reshape(-1), axis=1)
    fetched = lax.all_to_all(replies, "seq", split_axis=1, concat_axis=1, tiled=True)
    chosen = jnp.take(fetched, slot_index, axis=1).reshape(
        2, heads_dev, HD, blk_seq, degree * block_len
    )
    queries = query_cols.reshape(heads_dev, HD, blk_seq, block_len)
    scores = jnp.einsum(
        "hdbn,hdbj->hbnj", queries, chosen[0], preferred_element_type=jnp.float32
    ) * (1.0 / math.sqrt(HD))
    row_max = jnp.max(scores, -1, keepdims=True)
    weights = jnp.exp(scores - row_max)
    row_sum = jnp.sum(weights, -1)
    attended = jnp.einsum(
        "hbnj,hdbj->hdbn",
        weights.astype(jnp.bfloat16),
        chosen[1],
        preferred_element_type=jnp.float32,
    )
    return (attended / row_sum[:, None]).astype(jnp.bfloat16).reshape(feat_dev, node_seq)


def shards(
    query_cols,
    key_cols,
    value_cols,
    block_list,
    residual,
    out_proj,
    norm_gain,
    router_weight,
    expert_ids,
    expert_in,
    expert_out,
    cotangent,
):
    exp_count = lax.axis_size("expert")
    attended = attention(query_cols, key_cols, value_cols, block_list)
    feat_dev, node_seq = attended.shape
    tok_dev = node_seq // exp_count
    head_rows = lax.dynamic_slice_in_dim(out_proj, lax.axis_index("expert") * feat_dev, feat_dev, 0)
    projected = lax.psum_scatter(
        jnp.einsum("fn,fe->ne", attended, head_rows, preferred_element_type=jnp.float32),
        "expert",
        scatter_dimension=0,
        tiled=True,
    )
    stream = (residual.astype(jnp.float32) + projected).astype(jnp.bfloat16)
    stream_float = stream.astype(jnp.float32)
    inverse_rms = lax.rsqrt(jnp.mean(stream_float * stream_float, -1, keepdims=True) + norm_eps)
    normed = (stream_float * inverse_rms * norm_gain).astype(jnp.bfloat16)
    logits = jnp.dot(normed, router_weight, preferred_element_type=jnp.float32)
    expert_total = router_weight.shape[1]
    topk_count = expert_ids.shape[1]
    feature_width = normed.shape[1]
    id_hot = expert_ids[:, :, None] == jnp.arange(expert_total, dtype=jnp.int32)[None, None, :]
    gate_values = jax.nn.sigmoid(jnp.sum(jnp.where(id_hot, logits[:, None, :], 0.0), -1))
    flat_hot = id_hot.reshape(tok_dev * topk_count, expert_total).astype(jnp.int32)
    slot_rank = jnp.sum((jnp.cumsum(flat_hot, 0) - flat_hot) * flat_hot, 1)
    flat_ids = expert_ids.reshape(-1)
    exp_dev = expert_total // exp_count
    capacity = 2 * tok_dev * topk_count // expert_total
    position = (flat_ids % exp_dev * exp_count + flat_ids // exp_dev) * capacity + slot_rank
    buffer_rows = exp_dev * exp_count * capacity

    def pack_rows(source_rows):
        filled = jnp.zeros((buffer_rows, feature_width), jnp.bfloat16).at[position].set(source_rows)
        return filled.reshape(exp_dev, exp_count, capacity, feature_width)

    def unpack_rows(buffer):
        return jnp.take(buffer.reshape(buffer_rows, feature_width), position, axis=0).reshape(
            tok_dev, topk_count, feature_width
        )

    cot_float = cotangent.astype(jnp.float32)
    sent_rows = pack_rows(jnp.repeat(normed, topk_count, 0))
    scaled = (
        (gate_values[:, :, None] * cot_float[:, None, :])
        .astype(jnp.bfloat16)
        .reshape(tok_dev * topk_count, feature_width)
    )
    arrived = lax.all_to_all(sent_rows, "expert", split_axis=1, concat_axis=1, tiled=True)
    rows_in = arrived.reshape(exp_dev, exp_count * capacity, feature_width)
    preact = jnp.einsum("jrd,jdf->jrf", rows_in, expert_in, preferred_element_type=jnp.float32)
    hidden = gelu_value(preact).astype(jnp.bfloat16)
    produced = jnp.einsum(
        "jrf,jfd->jrd", hidden, expert_out, preferred_element_type=jnp.float32
    ).astype(jnp.bfloat16)
    rows_in, preact, hidden, produced = (
        rows_in,
        preact,
        hidden,
        produced.reshape(exp_dev, exp_count, capacity, feature_width),
    )
    produced_home = lax.all_to_all(produced, "expert", split_axis=1, concat_axis=1, tiled=True)
    arrived_cot = lax.all_to_all(
        pack_rows(scaled), "expert", split_axis=1, concat_axis=1, tiled=True
    )
    cot_rows = arrived_cot.reshape(exp_dev, exp_count * capacity, feature_width)
    grad_out = jnp.einsum("jrf,jrd->jfd", hidden, cot_rows, preferred_element_type=jnp.float32)
    grad_hidden = jnp.einsum(
        "jrd,jfd->jrf", cot_rows, expert_out, preferred_element_type=jnp.float32
    )
    grad_pre = (grad_hidden * gelu_slope(preact)).astype(jnp.bfloat16)
    grad_in = jnp.einsum("jrd,jrf->jdf", rows_in, grad_pre, preferred_element_type=jnp.float32)
    grad_back = jnp.einsum(
        "jrf,jdf->jrd", grad_pre, expert_in, preferred_element_type=jnp.float32
    ).astype(jnp.bfloat16)
    grad_in, grad_out, grad_back = (
        grad_in,
        grad_out,
        grad_back.reshape(exp_dev, exp_count, capacity, feature_width),
    )
    back_home = lax.all_to_all(grad_back, "expert", split_axis=1, concat_axis=1, tiled=True)
    grad_w_in, grad_w_out = lax.psum((grad_in, grad_out), "seq")
    expert_rows = unpack_rows(produced_home).astype(jnp.float32)
    layer_out = (stream_float + jnp.sum(gate_values[:, :, None] * expert_rows, 1)).astype(
        jnp.bfloat16
    )
    grad_gate = jnp.sum(cot_float[:, None, :] * expert_rows, -1)
    grad_logit = grad_gate * gate_values * (1.0 - gate_values)
    logit_table = jnp.sum(jnp.where(id_hot, grad_logit[:, :, None], 0.0), 1)
    router_term = jnp.dot(
        logit_table, router_weight.astype(jnp.float32).T, precision=lax.Precision.HIGHEST
    )
    grad_normed = jnp.sum(unpack_rows(back_home).astype(jnp.float32), 1) + router_term
    gained = grad_normed * norm_gain
    grad_stream = (
        cot_float
        + inverse_rms * gained
        - stream_float * inverse_rms**3 * jnp.mean(stream_float * gained, -1, keepdims=True)
    )
    return (layer_out, grad_stream.astype(jnp.bfloat16), grad_w_in, grad_w_out)


def solution(mesh):
    return jax.shard_map(
        shards,
        mesh=mesh,
        in_specs=(
            P("expert", "seq"),
            P("expert", "seq"),
            P("expert", "seq"),
            P("seq", None),
            P(("seq", "expert"), None),
            P(),
            P(),
            P(),
            P(("seq", "expert"), None),
            P("expert", None, None),
            P("expert", None, None),
            P(("seq", "expert"), None),
        ),
        out_specs=(
            P(("seq", "expert"), None),
            P(("seq", "expert"), None),
            P("expert", None, None),
            P("expert", None, None),
        ),
        check_vma=False,
    )
```

profile of v0, /device:TPU:1, one launch (start us, length us, event | category | flops | bytes accessed | tf_op | source)
XLA Modules:
  0.0 437.5 jit_solution(3616378894034025716)
XLA Ops:
  7.2 0.8 broadcast_multiply_fusion
  8.8 0.8 scatter_custom_fusion
  9.6 0.8 all_to_all.21
  10.4 11.6 %all-to-all-start = ((s32[64,1,2]{2,1,0:T(1,128)}), s32[64,1,2]{2,1,0:T(1,128)S(1)}, u32[]{:S(2)}, u32[]{:S(2)}) async-start(s32[64,1,2]{2,1,0:T(1,128)} %bitcast.2), calls=%async_computation | async-start | bytes 65536 | tf_op jit(solution)/shard_map/all_to_all | solution.py:45
  22.0 1.0 copy_bitcast_fusion
  23.0 8.3 %all-to-all-done = s32[64,1,2]{2,1,0:T(1,128)S(1)} async-done(((s32[64,1,2]{2,1,0:T(1,128)}), s32[64,1,2]{2,1,0:T(1,128)S(1)}, u32[]{:S(2)}, u32[]{:S(2)}) %all-to-all-start) | async-done | bytes 544 | tf_op jit(solution)/shard_map/all_to_all | solution.py:45
  31.5 0.5 broadcast.373
  32.0 0.7 reduce.12
  32.9 1.0 gather_fusion
  33.8 1.6 select_bitcast_fusion
  35.5 4.8 %all-to-all-start.1 = ((bf16[64,128,128]{2,0,1:T(8,128)(2,1)}), bf16[64,128,128]{2,0,1:T(8,128)(2,1)S(1)}, u32[]{:S(2)}, u32[]{:S(2)}) async-start(bf16[64,128,128]{2,0,1:T(8,128)(2,1)} %select_bitcast_fusion), calls=%async_computation.1 | async-start | bytes 4194304 | tf_op jit(solution)/shard_map/all_to_all | solution.py:52
  40.4 49.9 %all-to-all-done.1 = bf16[64,128,128]{2,0,1:T(8,128)(2,1)S(1)} async-done(((bf16[64,128,128]{2,0,1:T(8,128)(2,1)}), bf16[64,128,128]{2,0,1:T(8,128)(2,1)S(1)}, u32[]{:S(2)}, u32[]{:S(2)}) %all-to-all-start.1) | async-done | bytes 2097184 | tf_op jit(solution)/shard_map/all_to_all | solution.py:52
  90.3 1.6 gather_fusion.1
  91.9 1.4 select_bitcast_fusion.1
  93.4 0.2 copy.127
  93.6 0.3 reshape.371
  93.9 0.2 copy.126
  94.1 0.3 reshape.370
  94.5 1.0 bitcast_reduce_fusion
  95.5 0.7 fusion.1
  96.2 1.3 fusion.24
  97.6 2.6 fusion.43
  100.8 1.2 reduce-window.6
  102.0 0.2 slice_reduce_fusion
  102.4 40.5 %reduce-scatter.2.cloned.1.call-done = f32[256,256]{1,0:T(8,128)} async-done(((f32[2048,256]{1,0:T(8,128)}), f32[256,256]{1,0:T(8,128)}) %reduce-scatter.2.cloned.1.call-update) | async-done | bytes 262160 | tf_op jit(solution)/shard_map/reduce_scatter | solution.py:91
  142.9 1.1 fusion.30
  144.0 0.6 multiply_multiply_fusion.1
  145.0 2.7 scatter_custom_fusion.1
  147.7 16.6 %all_to_all.34 = bf16[2,8,64,256]{3,2,0,1:T(8,128)(2,1)S(1)} all-to-all(bf16[2,8,64,256]{3,2,0,1:T(8,128)(2,1)S(1)} %copy.138), channel_id=1, replica_groups=mesh['seq'=64,'expert'=8] {'expert'}, dimensions={1} | all-to-all | bytes 1048576 | tf_op jit(solution)/shard_map/all_to_all | solution.py:131
  164.4 0.4 fusion.72
  164.9 0.8 convolution_convert_fusion.1
  165.7 0.5 copy-done.1
  166.2 0.8 copy.140
  167.0 3.5 all-to-all-start.3
  170.7 0.4 mul.254
  171.3 11.4 %all-to-all-done.3 = bf16[2,8,64,256]{3,2,0,1:T(8,128)(2,1)S(1)} async-done(((bf16[2,8,64,256]{3,2,0,1:T(8,128)(2,1)}), bf16[2,8,64,256]{3,2,0,1:T(8,128)(2,1)S(1)}, u32[]{:S(2)}, u32[]{:S(2)}) %all-to-all-start.3) | async-done | bytes 524320 | tf_op jit(solution)/shard_map/all_to_all | solution.py:144
  182.8 2.0 gather_fusion.2
  184.7 0.2 multiply_reduce_fusion
  185.2 0.6 subtract_multiply_fusion
  186.1 0.5 copy-done.3
  186.6 3.2 scatter_custom_fusion.2
  189.9 1.2 copy.143
  191.1 14.6 %all_to_all.35 = bf16[2,8,64,256]{3,2,0,1:T(8,128)(2,1)S(1)} all-to-all(bf16[2,8,64,256]{3,2,0,1:T(8,128)(2,1)S(1)} %copy.143), channel_id=1, replica_groups=mesh['seq'=64,'expert'=8] {'expert'}, dimensions={1} | all-to-all | bytes 1048576 | tf_op jit(solution)/shard_map/all_to_all | solution.py:145
  205.7 1.4 fusion.9
  207.2 1.0 copy-done.6
  208.2 0.5 convolution_convert_fusion
  208.6 0.8 copy.145
  209.5 4.2 all-to-all-start.5
  213.6 0.3 all-reduce.3.cloned.1.call-start
  213.9 0.8 select_reduce_fusion
  214.7 2.7 fusion.73
  217.4 1.9 fusion.69
  219.3 6.5 %all-to-all-done.5 = bf16[2,8,64,256]{3,2,0,1:T(8,128)(2,1)} async-done(((bf16[2,8,64,256]{3,2,0,1:T(8,128)(2,1)}), bf16[2,8,64,256]{3,2,0,1:T(8,128)(2,1)}, u32[]{:S(2)}, u32[]{:S(2)}) %all-to-all-start.5) | async-done | bytes 524320 | tf_op jit(solution)/shard_map/all_to_all | solution.py:163
  225.8 1.1 copy.146
  226.9 2.0 gather_fusion.3
  229.0 0.3 reshape.385
  229.4 0.3 reshape.386
  229.7 0.6 reduce_sum.104
  230.3 0.7 multiply_reduce_fusion.1
  231.0 0.4 fusion.37
  231.5 0.8 fusion.36
  232.3 195.0 %all-reduce.3.cloned.1.call-done = (f32[2,256,512]{2,1,0:T(8,128)}, f32[2,512,256]{2,1,0:T(8,128)}) async-done(((f32[2,256,512]{2,1,0:T(8,128)}, f32[2,512,256]{2,1,0:T(8,128)}), (f32[2,256,512]{2,1,0:T(8,128)}, f32[2,512,256]{2,1,0:T(8,128)})) %all-reduce.3.cloned.1.call-update) | async-done | bytes 2097168 | tf_op jit(solution)/shard_map/psum | solution.py:164
  427.3 2.4 copy.179
  429.6 1.0 copy.180
  (100 shorter events, 3.7 us)
Async XLA Ops:
  7.2 157.7 %copy-start = (bf16[2,512,256]{2,1,0:T(8,128)(2,1)S(1)}, bf16[2,512,256]{2,1,0:T(8,128)(2,1)}, u32[]{:S(2)}) copy-start(bf16[2,512,256]{2,1,0:T(8,128)(2,1)} %param.24) | copy-start | bytes 1572868
  10.4 20.9 %all-to-all-start = ((s32[64,1,2]{2,1,0:T(1,128)}), s32[64,1,2]{2,1,0:T(1,128)S(1)}, u32[]{:S(2)}, u32[]{:S(2)}) async-start(s32[64,1,2]{2,1,0:T(1,128)} %bitcast.2), calls=%async_computation | async-start | bytes 65536 | tf_op jit(solution)/shard_map/all_to_all | solution.py:45
  35.5 54.8 %all-to-all-start.1 = ((bf16[64,128,128]{2,0,1:T(8,128)(2,1)}), bf16[64,128,128]{2,0,1:T(8,128)(2,1)S(1)}, u32[]{:S(2)}, u32[]{:S(2)}) async-start(bf16[64,128,128]{2,0,1:T(8,128)(2,1)} %select_bitcast_fusion), calls=%async_computation.1 | async-start | bytes 4194304 | tf_op jit(solution)/shard_map/all_to_all | solution.py:52
  40.3 102.6 %reduce-scatter.2.cloned.1.call-start = ((), (), s32[]{:S(2)}) async-start(), calls=%async_computation.7 | async-start | bytes 2359296 | tf_op jit(solution)/shard_map/reduce_scatter | solution.py:91
  93.4 1.1 copy-start.13
  97.6 2.6 copy-start.17
  97.6 45.3 %copy-start.14 = (bf16[256,256]{1,0:T(8,128)(2,1)S(1)}, bf16[256,256]{1,0:T(8,128)(2,1)}, u32[]{:S(2)}) copy-start(bf16[256,256]{1,0:T(8,128)(2,1)} %param.18) | copy-start | bytes 393220
  100.2 44.4 %copy-start.24 = (f32[256]{0:T(256)S(1)}, f32[256]{0:T(256)}, u32[]{:S(2)}) copy-start(f32[256]{0:T(256)} %param.20) | copy-start | bytes 3076
  144.6 19.8 %copy-start.20 = (f32[256]{0:T(256)}, f32[256]{0:T(256)S(1)}, u32[]{:S(2)}) copy-start(f32[256]{0:T(256)S(1)} %get-tuple-element.21) | copy-start | bytes 3076
  144.8 19.5 %copy-start.11 = (bf16[2,256,512]{2,1,0:T(8,128)(2,1)S(1)}, bf16[2,256,512]{2,1,0:T(8,128)(2,1)}, u32[]{:S(2)}) copy-start(bf16[2,256,512]{2,1,0:T(8,128)(2,1)} %param.23) | copy-start | bytes 1572868
  164.8 1.4 copy-start.1
  166.2 4.3 copy-start.7
  166.2 4.9 %copy-start.15 = (bf16[256,16]{0,1:T(8,128)(2,1)S(1)}, bf16[256,16]{0,1:T(8,128)(2,1)}, u32[]{:S(2)}) copy-start(bf16[256,16]{0,1:T(8,128)(2,1)} %param.21) | copy-start | bytes 24580
  167.0 15.7 %all-to-all-start.3 = ((bf16[2,8,64,256]{3,2,0,1:T(8,128)(2,1)}), bf16[2,8,64,256]{3,2,0,1:T(8,128)(2,1)S(1)}, u32[]{:S(2)}, u32[]{:S(2)}) async-start(bf16[2,8,64,256]{3,2,0,1:T(8,128)(2,1)} %copy.140), calls=%async_computation.4 | async-start | bytes 1048576 | tf_op jit(solution)/shard_map/all_to_all | solution.py:144
  171.1 13.9 %copy-start.22 = (pred[512]{0:T(512)(128)(4,1)}, pred[512]{0:T(512)(128)(4,1)S(1)}, u32[]{:S(2)}) copy-start(pred[512]{0:T(512)(128)(4,1)S(1)} %get-tuple-element.9) | copy-start | bytes 1540
  171.1 13.9 %copy-start.18 = (s32[1024]{0:T(1024)}, s32[1024]{0:T(1024)S(1)}, u32[]{:S(2)}) copy-start(s32[1024]{0:T(1024)S(1)} %pad_clamp_fusion) | copy-start | bytes 12292
  186.0 0.7 copy-start.3
  189.9 15.8 %copy-start.2 = (f32[2,512,512]{2,1,0:T(8,128)S(1)}, f32[2,512,512]{2,1,0:T(8,128)}, u32[]{:S(2)}) copy-start(f32[2,512,512]{2,1,0:T(8,128)} %copy-done.1) | copy-start | bytes 6291460
  205.7 1.5 copy-start.9
  205.7 2.5 copy-start.12
  207.2 1.0 copy-start.6
  209.5 16.3 %all-to-all-start.5 = ((bf16[2,8,64,256]{3,2,0,1:T(8,128)(2,1)}), bf16[2,8,64,256]{3,2,0,1:T(8,128)(2,1)}, u32[]{:S(2)}, u32[]{:S(2)}) async-start(bf16[2,8,64,256]{3,2,0,1:T(8,128)(2,1)} %copy.145), calls=%async_computation.6 | async-start | bytes 1048576 | tf_op jit(solution)/shard_map/all_to_all | solution.py:163
  213.6 213.7 %all-reduce.3.cloned.1.call-start = ((), (), s32[]{:S(2)}) async-start(), calls=%async_computation.8 | async-start | bytes 4194304 | tf_op jit(solution)/shard_map/psum | solution.py:164
  213.9 3.5 copy-start.10
  219.3 7.6 %copy-start.19 = (s32[1024]{0:T(1024)S(1)}, s32[1024]{0:T(1024)}, u32[]{:S(2)}) copy-start(s32[1024]{0:T(1024)} %copy-done.18) | copy-start | bytes 12292
  219.3 9.5 %copy-start.23 = (pred[512]{0:T(512)(128)(4,1)S(1)}, pred[512]{0:T(512)(128)(4,1)}, u32[]{:S(2)}) copy-start(pred[512]{0:T(512)(128)(4,1)} %copy-done.22) | copy-start | bytes 1540
  228.8 1.5 copy-start.4
  229.0 2.0 copy-start.16
  229.0 2.0 copy-start.25
  229.0 2.4 copy-start.8
  229.0 2.4 copy-start.21
  229.0 2.4 copy-start.26
  427.3 2.4 copy-start.5
Sparse Core Ops, SparseCore 0:
  100.4 42.4 reduce-scatter.1
  219.4 207.8 all-reduce.2
where the time goes:
time: 440 us; the launch traced here: 437 us
  waiting for transfers between devices  312 us (71%)
  blocking collectives  31.2 us (7%)
  local copies, waits for them, and re-layouts  25.4 us (6%)
  starting transfers between devices  24.4 us (6%)
  other arithmetic  16.9 us (4%)
  between operations  14.8 us (3%)
  matrix products  13.2 us (3%)
    psum x1, waiting for transfers between devices, shards(): grad_w_in, grad_w_out = lax.psum((grad_in, grad_out), 'seq')  195 us
    all_to_all x1, waiting for transfers between devices, attention(): lax.all_to_all(replies, 'seq', split_axis=1, concat_axis=1, tiled=True)  49.9 us
    reduce_scatter x1, waiting for transfers between devices, shards(): lax.psum_scatter(jnp.einsum('fn,fe->ne', attended, head_rows, preferred_e...  40.5 us
    all_to_all x1, blocking collectives, shards(): lax.all_to_all(sent_rows, 'expert', split_axis=1, concat_axis=1, tiled=True)  16.6 us
    all_to_all x1, blocking collectives, shards(): lax.all_to_all(pack_rows(scaled), 'expert', split_axis=1, concat_axis=1,...  14.6 us
    all_to_all x1, starting transfers between devices, attention(): lax.all_to_all(wanted.reshape(seq_count, capacity), 'seq', split_axis=0,...  11.6 us
    all_to_all x1, waiting for transfers between devices, shards(): lax.all_to_all(produced, 'expert', split_axis=1, concat_axis=1, tiled=True)  11.4 us
  transfers between devices with their start and end apart: 6, of which 6 were waited for; matrix products, arithmetic and copies ran while one was open for 4% of the time, Pallas kernels for 0%

commit v1 on v0

v1 whole, which is shorter than its diff:
```python
import math

import jax
import jax.numpy as jnp
from jax import lax
from jax.experimental import pallas as pl
from jax.experimental.pallas import tpu as pltpu
from jax.sharding import PartitionSpec as P

MESH = pl.DeviceIdType.MESH
BF = jnp.bfloat16
F32 = jnp.float32
HD = 32
NY, NX, NC, NZ = 8, 4, 2, 8
CAPE = 64

norm_eps = 1e-05
root_two_pi = 0.7978845608028654
cubic_term = 0.044715

TN = (((0,), (0,)), ((), ()))
NT = (((1,), (1,)), ((), ()))


def dot(a, b, dims=(((1,), (0,)), ((), ()))):
    return lax.dot_general(a, b, dims, preferred_element_type=F32)


def place():
    seq, z = lax.axis_index("seq"), lax.axis_index("expert")
    y = seq // (NX * NC)
    x = (seq // NC) % NX
    c = seq % NC
    return y, x, c, z


def device(y, x, c, z):
    return ((y * NX + x) * NC + c, z)


def send(src, dst, ssem, rsem, dev):
    copy = pltpu.make_async_remote_copy(
        src_ref=src, dst_ref=dst, send_sem=ssem, recv_sem=rsem, device_id=dev, device_id_type=MESH
    )
    copy.start()
    return copy


class Ring:
    def __init__(self, slots, ssem, rsem, up, down, far_up):
        self.slots, self.ssem, self.rsem = slots, ssem, rsem
        self.up, self.down, self.far_up = up, down, far_up
        self.copies = {}

    def go(self, frm, to, dev):
        self.copies[to] = send(self.slots(frm), self.slots(to), self.ssem(to), self.rsem(to), dev)

    def begin(self):
        self.go(0, 1, self.up)
        self.go(0, 7, self.down)

    def arrive(self, k):
        self.copies[k].wait_recv()
        if k < 3 or (k == 3 and self.far_up):
            self.go(k, k + 1, self.up)
        if k > 5 or (k == 5 and not self.far_up):
            self.go(k, k - 1, self.down)

    def finish(self):
        for copy in self.copies.values():
            copy.wait_send()


def exchange_kernel(
    idx, wtab, kv, q, res, cot, ids,
    att_all, res_all, cot_all, ids_all,
    yb1, yb2, yb3, yb4, yb5, yb6, yb7,
    zr, zc, zi, wr, wsm, sb, rv, at,
    y_s, y_r, z_s, z_r, w_s, w_r, x_s, x_r, a_s, a_r, l_s,
):
    y, x, c, z = place()
    up_y, down_y = device((y + 1) % NY, x, c, z), device((y + 7) % NY, x, c, z)
    up_z, down_z = device(y, x, c, (z + 1) % NZ), device(y, x, c, (z + 7) % NZ)
    row = [(dx, dc) for dx in range(NX) for dc in range(NC)]
    peers = [device(y, (x + dx) % NX, (c + dc) % NC, z) for dx, dc in row]

    barrier = pltpu.get_barrier_semaphore()
    for dev in [up_y, down_y, up_z, down_z] + peers[1:]:
        pl.semaphore_signal(barrier, inc=1, device_id=dev, device_id_type=MESH)
    pl.semaphore_wait(barrier, 11)

    ybs = [kv, yb1, yb2, yb3, yb4, yb5, yb6, yb7]
    tables = [
        send(wtab, wr.at[r], w_s.at[r], w_r.at[r], peers[r]) for r in range(1, 8)
    ]

    def y_ring(ch):
        return Ring(
            lambda k: ybs[k].at[pl.ds(ch * 8, 8)],
            lambda k: y_s.at[ch, k],
            lambda k: y_r.at[ch, k],
            up_y, down_y, ch == 0,
        )

    def z_ring(i, own, buf, far_up):
        return Ring(
            lambda k: own if k == 0 else buf.at[k],
            lambda k: z_s.at[i, k],
            lambda k: z_r.at[i, k],
            up_z, down_z, far_up,
        )

    ys = [y_ring(0), y_ring(1)]
    zs = [z_ring(0, res, zr, True), z_ring(1, cot, zc, False), z_ring(2, ids, zi, True)]
    zs[2].begin()
    for ch in range(2):
        ys[ch].begin()
        zs[ch].begin()

    own_table = pltpu.make_async_copy(wtab, wsm.at[0], l_s.at[0])
    own_table.start()
    for r in range(1, 8):
        tables[r - 1].wait_recv()
    rest = pltpu.make_async_copy(wr.at[pl.ds(1, 7)], wsm.at[pl.ds(1, 7)], l_s.at[1])
    rest.start()
    own_table.wait()
    rest.wait()

    line = x * NC + c
    moved = []

    def pick(rel):
        source = ybs[(8 - rel) % 8]
        owner_row = (y + rel) % NY
        for r, (dx, dc) in enumerate(row):
            asked = ((NX - dx) % NX) * NC + dc
            for s in range(2):
                block = wsm[asked, owner_row, line * 2 + s]
                if r == 0:
                    rv[rel * 2 + s] = source[block]
                else:
                    sb[rel, r, s] = source[block]
            if r:
                moved.append(
                    send(
                        sb.at[rel, r],
                        rv.at[pl.ds((r * 8 + rel) * 2, 2)],
                        x_s.at[r, rel],
                        x_r.at[r, rel],
                        peers[r],
                    )
                )

    pick(0)
    res_all[0] = res[...]
    cot_all[0] = cot[...]
    ids_all[0] = ids[...]
    for k in (1, 2, 3):
        for ch in range(2):
            for slot in (k, 8 - k):
                ys[ch].arrive(slot)
                zs[ch].arrive(slot)
        for slot in (k, 8 - k):
            zs[2].arrive(slot)
            pick((8 - slot) % 8)
            res_all[slot] = zr[slot]
            cot_all[slot] = zc[slot]
            ids_all[slot] = zi[slot]
    for ring in ys + zs:
        ring.arrive(4)
    pick(4)
    res_all[4] = zr[4]
    cot_all[4] = zc[4]
    ids_all[4] = zi[4]
    for copy in moved:
        copy.wait_recv()

    rings = []

    def attend(ch):
        def block(i, carry):
            b = ch * 4 + i
            pairs = [rv[idx[b * 4 + j]] for j in range(4)]
            keys = jnp.concatenate([p[:HD] for p in pairs], 1)
            values = jnp.concatenate([p[HD:] for p in pairs], 1)
            queries = q[:, pl.ds(pl.multiple_of(b * 128, 128), 128)]
            scores = dot(keys, queries, TN) * (1.0 / math.sqrt(HD))
            weights = jnp.exp(scores - jnp.max(scores, 0, keepdims=True))
            total = jnp.sum(weights, 0, keepdims=True)
            out = dot(values, weights.astype(BF)) / total
            at[0, ch, :, pl.ds(pl.multiple_of(i * 128, 128), 128)] = out.astype(BF)
            return carry

        lax.fori_loop(0, 4, block, 0)
        ring = Ring(
            lambda k: at.at[k, ch],
            lambda k: a_s.at[ch, k],
            lambda k: a_r.at[ch, k],
            up_z, down_z, ch < 2,
        )
        ring.begin()
        rings.append(ring)

    def keep(k, ch):
        head = (z + NZ - k) % NZ
        att_all[pl.ds(pl.multiple_of(head * HD, HD), HD), ch * 512 : (ch + 1) * 512] = at[k, ch]

    for ch in range(4):
        attend(ch)
    for ch in range(4):
        keep(0, ch)
    for k in (1, 2, 3):
        for ch in range(4):
            for slot in (k, 8 - k):
                rings[ch].arrive(slot)
        for ch in range(4):
            for slot in (k, 8 - k):
                keep(slot, ch)
    for ch in range(4):
        rings[ch].arrive(4)
        keep(4, ch)
    for ring in ys + zs + rings:
        ring.finish()
    for copy in tables + moved:
        copy.wait_send()


def expert_kernel(
    att, res, cot, ids, out_proj, gain, router, w_in, w_out,
    grads, layer_out, grad_stream,
    rows, cots, gates, ga, gb, ret, rr, hot_own, rank_own, stream_own, inv_own,
    rc, t1, rx, t2, ry, full,
    r_s, r_r, c_s, c_r, x_s, x_r, y_s, y_r, gy_s, gy_r, gx_s, gx_r, gc_s, gc_r,
):
    y, x, c, z = place()
    partner = device(y, x, 1 - c, z)
    x_dev = [device(y, (x + d) % NX, c, z) for d in range(NX)]
    y_dev = [device((y + d) % NY, x, c, z) for d in range(NY)]
    z_dev = [device(y, x, c, (z + NZ - d) % NZ) for d in range(NZ)]
    barrier = pltpu.get_barrier_semaphore()
    for dev in [partner] + x_dev[1:] + y_dev[1:] + z_dev[1:]:
        pl.semaphore_signal(barrier, inc=1, device_id=dev, device_id_type=MESH)

    expert_row = lax.broadcasted_iota(jnp.int32, (16, 256), 0)
    before = (
        lax.broadcasted_iota(jnp.int32, (256, 256), 0)
        < lax.broadcasted_iota(jnp.int32, (256, 256), 1)
    ).astype(F32).astype(BF)
    slot_row = lax.broadcasted_iota(jnp.int32, (CAPE, 256), 0).astype(F32)

    def one_row(table, e):
        return jnp.sum(jnp.where(expert_row == e, table, 0.0), 0, keepdims=True)

    def selector(hot, rank, e):
        return jnp.where(
            (slot_row == one_row(rank, e)) & (one_row(hot, e) > 0.5), 1.0, 0.0
        )

    def local(j):
        return 1 - c if j == 0 else c

    def home(k, carry):
        owner = (z + NZ - k) % NZ
        mine = att[:, pl.ds(pl.multiple_of(owner * 256, 256), 256)]
        stream = (res[k].astype(F32) + dot(mine, out_proj[...], TN)).astype(BF)
        wide = stream.astype(F32)
        inv = lax.rsqrt(jnp.mean(wide * wide, -1, keepdims=True) + norm_eps)
        normed = (wide * inv * gain[...]).astype(BF)
        gate = jax.nn.sigmoid(dot(router[...], normed, NT))
        listed = ids[k]
        hot = jnp.where(
            (listed[0:1] == expert_row) | (listed[1:2] == expert_row), 1.0, 0.0
        )
        rank = dot(hot.astype(BF), before)

        @pl.when(k == 0)
        def _():
            hot_own[...] = hot
            rank_own[...] = rank
            stream_own[...] = wide
            inv_own[...] = jnp.broadcast_to(inv, (256, 128))

        at = pl.ds(pl.multiple_of(k * CAPE, CAPE), CAPE)
        for j in range(2):
            e = 2 * z + local(j)
            picked = selector(hot, rank, e)
            picked_b = picked.astype(BF)
            rows[j, at, :] = dot(picked_b, normed).astype(BF)
            cots[j, at, :] = dot(picked_b, cot[k]).astype(BF)
            value = jnp.sum(picked * one_row(gate, e), 1, keepdims=True)
            gates[j, at, :] = jnp.broadcast_to(value, (CAPE, 128))
        return carry

    lax.fori_loop(0, NZ, home, 0)

    back = []
    for j in range(2):
        e = local(j)
        inp, outp = w_in[e], w_out[e]
        x_rows = rows[j]
        gate = gates[j][:, 0:1]
        cot_rows = cots[j].astype(F32)
        scaled = (gate * cot_rows).astype(BF)
        pre = dot(x_rows, inp)
        square = pre * pre
        t = jnp.tanh(root_two_pi * (pre + cubic_term * square * pre))
        hidden = (0.5 * pre * (1.0 + t)).astype(BF)
        slope = 0.5 * (1.0 + t) + 0.5 * pre * (1.0 - t * t) * root_two_pi * (
            1.0 + 3.0 * cubic_term * square
        )
        grad_pre = (dot(scaled, outp, NT) * slope).astype(BF)
        gb[j] = dot(hidden, scaled, TN).astype(BF)
        grad_in = dot(x_rows, grad_pre, TN).astype(BF)
        ga[j, 0:256, :] = grad_in[:, 0:256]
        ga[j, 256:512, :] = grad_in[:, 256:512]
        if j == 0:
            pl.semaphore_wait(barrier, 18)
            pair = [
                send(g.at[0], rc.at[i], c_s.at[i], c_r.at[i], partner)
                for i, g in enumerate((ga, gb))
            ]
        made = dot(hidden, outp)
        grad_rows = dot(grad_pre, inp, NT)
        grad_gate = jnp.sum(cot_rows * made, -1, keepdims=True)
        grad_logit = grad_gate * gate * (1.0 - gate)
        column = one_row(router[...].astype(F32), 2 * z + e)
        first = (gate * made).astype(BF)
        second = (grad_rows + grad_logit * column).astype(BF)
        for k in range(NZ):
            ret[j, k, :, 0:256] = first[k * CAPE : (k + 1) * CAPE]
            ret[j, k, :, 256:512] = second[k * CAPE : (k + 1) * CAPE]
        for k in (4, 3, 5, 2, 6, 1, 7):
            back.append(
                send(ret.at[j, k], rr.at[j, k], r_s.at[j, k], r_r.at[j, k], z_dev[k])
            )

    chains = range(2)
    sent = []
    over_x = [[], []]
    for i in chains:
        pair[i].wait_recv()
        own = ga if i == 0 else gb
        t1[i] = (own[1].astype(F32) + rc[i].astype(F32)).astype(BF)
        for d in (2, 1, 3):
            to = (x + d) % NX
            over_x[i].append(
                send(
                    t1.at[i, pl.ds(pl.multiple_of(to * 128, 128), 128)],
                    rx.at[i, d], x_s.at[i, d], x_r.at[i, d], x_dev[d],
                )
            )
    over_y = [[], []]
    for i in chains:
        total = t1[i, pl.ds(pl.multiple_of(x * 128, 128), 128), :].astype(F32)
        for copy in over_x[i]:
            copy.wait_recv()
        for d in range(1, NX):
            total += rx[i, d].astype(F32)
        t2[i] = total.astype(BF)
        for d in (4, 3, 5, 2, 6, 1, 7):
            to = (y + d) % NY
            over_y[i].append(
                send(
                    t2.at[i, pl.ds(pl.multiple_of(to * 16, 16), 16)],
                    ry.at[i, d], y_s.at[i, d], y_r.at[i, d], y_dev[d],
                )
            )
    def span(size):
        first = {16: x * 128 + y * 16, 128: x * 128, 512: 0}[size] + c * 512
        return pl.ds(pl.multiple_of(first, size), size)

    out_y = [[], []]
    for i in chains:
        total = t2[i, pl.ds(pl.multiple_of(y * 16, 16), 16), :].astype(F32)
        for copy in over_y[i]:
            copy.wait_recv()
        for d in range(1, NY):
            total += ry[i, d].astype(F32)
        full[i, span(16), :] = total.astype(BF)
        for d in (4, 3, 5, 2, 6, 1, 7):
            part = full.at[i, span(16)]
            out_y[i].append(send(part, part, gy_s.at[i, d], gy_r.at[i, d], y_dev[d]))
    out_x = [[], []]
    for i in chains:
        for copy in out_y[i]:
            copy.wait_recv()
        for d in (2, 1, 3):
            part = full.at[i, span(128)]
            out_x[i].append(send(part, part, gx_s.at[i, d], gx_r.at[i, d], x_dev[d]))

    for copy in back:
        copy.wait_recv()
    hot, rank = hot_own[...], rank_own[...]
    total = None
    for j in range(2):
        picks, parts = [], []
        for k in range(NZ):
            e = 2 * ((z + k) % NZ) + local(j)
            picks.append(selector(hot, rank, e).astype(BF))
            parts.append(ret[j, 0] if k == 0 else rr[j, k])
        part = dot(jnp.concatenate(picks, 0), jnp.concatenate(parts, 0), TN)
        total = part if total is None else total + part
    wide, inv = stream_own[...], inv_own[...][:, 0:1]
    layer_out[...] = (wide + total[:, 0:256]).astype(BF)
    gained = total[:, 256:512] * gain[...]
    mean = jnp.mean(wide * gained, -1, keepdims=True)
    grad_stream[...] = (
        cot[0].astype(F32) + inv * gained - wide * (inv * inv * inv) * mean
    ).astype(BF)

    out_c = []
    for i in chains:
        for copy in out_x[i]:
            copy.wait_recv()
        part = full.at[i, span(512)]
        out_c.append(send(part, part, gc_s.at[i], gc_r.at[i], partner))
    for copy in out_c:
        copy.wait_recv()
    grads[...] = full[...]
    for copy in pair + back + out_c:
        copy.wait_send()
    for group in (over_x, over_y, out_y, out_x):
        for i in chains:
            for copy in group[i]:
                copy.wait_send()


VM = pl.BlockSpec(memory_space=pltpu.VMEM)
SM = pl.BlockSpec(memory_space=pltpu.SMEM)
DMA = pltpu.SemaphoreType.DMA


def exchange(idx, wtab, kv, q, res, cot, ids):
    return pl.pallas_call(
        exchange_kernel,
        name="exchange",
        out_shape=(
            jax.ShapeDtypeStruct((256, 2048), BF),
            jax.ShapeDtypeStruct((8, 256, 256), BF),
            jax.ShapeDtypeStruct((8, 256, 256), BF),
            jax.ShapeDtypeStruct((8, 8, 256), jnp.int32),
        ),
        in_specs=[SM] + [VM] * 6,
        out_specs=(VM,) * 4,
        scratch_shapes=[pltpu.VMEM((16, 64, 128), BF)] * 7
        + [
            pltpu.VMEM((8, 256, 256), BF),
            pltpu.VMEM((8, 256, 256), BF),
            pltpu.VMEM((8, 8, 256), jnp.int32),
            pltpu.VMEM((8, 8, 128), jnp.int32),
            pltpu.SMEM((8, 8, 128), jnp.int32),
            pltpu.VMEM((8, 8, 2, 64, 128), BF),
            pltpu.VMEM((128, 64, 128), BF),
            pltpu.VMEM((8, 4, 32, 512), BF),
            DMA((2, 8)), DMA((2, 8)), DMA((3, 8)), DMA((3, 8)),
            DMA((8,)), DMA((8,)), DMA((8, 8)), DMA((8, 8)),
            DMA((4, 8)), DMA((4, 8)), DMA((2,)),
        ],
        compiler_params=pltpu.CompilerParams(
            collective_id=0, has_side_effects=True, vmem_limit_bytes=40 << 20
        ),
    )(idx, wtab, kv, q, res, cot, ids)


def experts(*args):
    return pl.pallas_call(
        expert_kernel,
        name="experts",
        out_shape=(
            jax.ShapeDtypeStruct((2, 1024, 256), BF),
            jax.ShapeDtypeStruct((256, 256), BF),
            jax.ShapeDtypeStruct((256, 256), BF),
        ),
        in_specs=[VM] * 9,
        out_specs=(VM,) * 3,
        scratch_shapes=[
            pltpu.VMEM((2, 512, 256), BF),
            pltpu.VMEM((2, 512, 256), BF),
            pltpu.VMEM((2, 512, 128), F32),
            pltpu.VMEM((2, 512, 256), BF),
            pltpu.VMEM((2, 512, 256), BF),
            pltpu.VMEM((2, 8, CAPE, 512), BF),
            pltpu.VMEM((2, 8, CAPE, 512), BF),
            pltpu.VMEM((16, 256), F32),
            pltpu.VMEM((16, 256), F32),
            pltpu.VMEM((256, 256), F32),
            pltpu.VMEM((256, 128), F32),
            pltpu.VMEM((2, 512, 256), BF),
            pltpu.VMEM((2, 512, 256), BF),
            pltpu.VMEM((2, 4, 128, 256), BF),
            pltpu.VMEM((2, 128, 256), BF),
            pltpu.VMEM((2, 8, 16, 256), BF),
            pltpu.VMEM((2, 1024, 256), BF),
            DMA((2, 8)), DMA((2, 8)), DMA((2,)), DMA((2,)),
            DMA((2, 4)), DMA((2, 4)), DMA((2, 8)), DMA((2, 8)),
            DMA((2, 8)), DMA((2, 8)), DMA((2, 4)), DMA((2, 4)),
            DMA((2,)), DMA((2,)),
        ],
        compiler_params=pltpu.CompilerParams(
            collective_id=1, has_side_effects=True, vmem_limit_bytes=44 << 20
        ),
    )(*args)


def tables(block_list):
    y, x, c, _ = place()
    asked = block_list.reshape(-1)
    owner, inner = asked // 16, asked % 16
    entry = jnp.arange(64, dtype=jnp.int32)
    earlier = (owner[:, None] == owner[None, :]) & (entry[None, :] < entry[:, None])
    rank = jnp.sum(earlier.astype(jnp.int32), 1)
    owner_y, line = owner // (NX * NC), owner % (NX * NC)
    rows = jnp.arange(8, dtype=jnp.int32)[:, None, None]
    lanes = jnp.arange(128, dtype=jnp.int32)[None, :, None]
    hit = (owner_y[None, None, :] == rows) & ((line * 2 + rank)[None, None, :] == lanes)
    wanted = jnp.sum(jnp.where(hit, inner[None, None, :], 0), -1)
    supplier = (x - line // NC) % NX * NC + (c - line % NC) % NC
    index = (supplier * 8 + (owner_y - y) % NY) * 2 + rank
    return index, wanted


def shards(
    query_cols, key_cols, value_cols, block_list, residual, out_proj, norm_gain,
    router_weight, expert_ids, expert_in, expert_out, cotangent,
):
    index, wanted = tables(block_list)
    pairs = jnp.concatenate([key_cols, value_cols], 0).reshape(64, 16, 128)
    ids = jnp.pad(expert_ids.T, ((0, 6), (0, 0)))
    att, res, cot, listed = exchange(
        index, wanted, jnp.transpose(pairs, (1, 0, 2)), query_cols, residual, cotangent, ids
    )
    grads, layer_out, grad_stream = experts(
        att, res, cot, listed, out_proj, norm_gain.reshape(1, 256), router_weight.T,
        expert_in, expert_out,
    )
    wide = grads.astype(F32)
    grad_in = jnp.transpose(wide[0].reshape(2, 2, 256, 256), (0, 2, 1, 3)).reshape(2, 256, 512)
    return layer_out, grad_stream, grad_in, wide[1].reshape(2, 512, 256)


def solution(mesh):
    assert (mesh.shape["seq"], mesh.shape["expert"]) == (NY * NX * NC, NZ)
    return jax.shard_map(
        shards,
        mesh=mesh,
        in_specs=(
            P("expert", "seq"),
            P("expert", "seq"),
            P("expert", "seq"),
            P("seq", None),
            P(("seq", "expert"), None),
            P(),
            P(),
            P(),
            P(("seq", "expert"), None),
            P("expert", None, None),
            P("expert", None, None),
            P(("seq", "expert"), None),
        ),
        out_specs=(
            P(("seq", "expert"), None),
            P(("seq", "expert"), None),
            P("expert", None, None),
            P("expert", None, None),
        ),
        check_vma=False,
    )
```

time: 440 us -> 111 us (0.25)
  waiting for transfers between devices: 312 us -> 0 us
  Pallas kernels: 0 us -> 102 us
  blocking collectives: 31.2 us -> 0 us
  starting transfers between devices: 24.4 us -> 0 us
  local copies, waits for them, and re-layouts: 25.4 us -> 6.21 us
  other arithmetic: 16.9 us -> 1.58 us
  between operations: 14.8 us -> 0.86 us
  matrix products: 13.2 us -> 0 us
    psum x1 -> x0, waiting for transfers between devices: 195 us -> none  [shards(): grad_w_in, grad_w_out = lax.psum((grad_in, grad_out), 'seq')]
    pallas_call x0 -> x2, Pallas kernels: none -> 102 us  [the longest x1 63.6 us: exchange(): pl.pallas_call(exchange_kernel, name='exchange', out_shape=(jax.ShapeDtyp...]
    all_to_all x4 -> x0, waiting for transfers between devices: 76.1 us -> none  [the longest x1 49.9 us: attention(): lax.all_to_all(replies, 'seq', split_axis=1, concat_axis=1, tiled=True)]
    reduce_scatter x1 -> x0, waiting for transfers between devices: 40.5 us -> none  [shards(): lax.psum_scatter(jnp.einsum('fn,fe->ne', attended, head_rows, preferred_e...]
    all_to_all x2 -> x0, blocking collectives: 31.2 us -> none  [the longest x1 16.6 us: shards(): lax.all_to_all(sent_rows, 'expert', split_axis=1, concat_axis=1, tiled=True)]
    all_to_all x4 -> x0, starting transfers between devices: 24.1 us -> none  [the longest x1 11.6 us: attention(): lax.all_to_all(wanted.reshape(seq_count, capacity), 'seq', split_axis=0,...]
    dot_general x11 -> x0, matrix products: 13.2 us -> none  [the longest x1 2.68 us: shards(): jnp.einsum('jrd,jrf->jdf', rows_in, grad_pre, preferred_element_type=jnp....]
    gather x4 -> x0, local copies, waits for them, and re-layouts: 6.51 us -> none  [the longest x2 3.91 us: unpack_rows(): jnp.take(buffer.reshape(buffer_rows, feature_width), position, axis=0)]
  transfers between devices with their start and end apart: 6 -> 0, of which waited for: 6 -> 0; matrix products, arithmetic and copies ran while one was open for 4% -> 0% of each run, Pallas kernels for 0% -> 0%
where the time goes in v1:
time: 111 us
  Pallas kernels  102 us (92%)
  local copies, waits for them, and re-layouts  6.21 us (6%)
  other arithmetic  1.58 us (1%)
    pallas_call x1, Pallas kernels, exchange(): pl.pallas_call(exchange_kernel, name='exchange', out_shape=(jax.ShapeDtyp...  63.6 us
    pallas_call x1, Pallas kernels, experts(): pl.pallas_call(expert_kernel, name='experts', out_shape=(jax.ShapeDtypeSt...  38.2 us
    unnamed x23, local copies, waits for them, and re-layouts  3.86 us

profile of v1, /device:TPU:1, one launch (start us, length us, event | category | flops | bytes accessed | tf_op | source)
XLA Modules:
  0.0 110.5 jit_solution(11246124060099717458)
XLA Ops:
  0.6 0.0 copy-start.6
  0.7 0.0 copy-start.9
  0.7 0.0 copy-start.8
  0.7 0.0 copy-start.7
  0.7 0.0 copy-start.3
  0.7 0.6 copy-done.8
  1.4 0.1 copy.21
  1.4 0.1 reshape.210
  1.5 0.2 convert_reduce_fusion
  1.8 0.1 iota_compare_fusion
  1.9 0.2 select_reduce_fusion.wtab
  2.0 0.0 copy-done.9
  2.0 0.0 copy-start
  2.1 0.0 copy-start.1
  2.1 1.1 %bitcast_bitcast_fusion.kv = bf16[16,64,128]{2,1,0:T(8,128)(2,1)S(1)} fusion(bf16[32,2048]{1,0:T(8,128)(2,1)} %param.14, bf16[32,2048]{1,0:T(8,128)(2,1)} %param.13), kind=kLoop, calls=%fused_computation | loop fusion | flops 524288 | bytes 524288 | tf_op jit(solution)/shard_map/transpose | solution.py:530
  3.2 0.0 copy-done.3
  3.2 0.0 copy-start.4
  3.2 0.9 copy-done.4
  4.1 0.0 copy-start.5
  4.1 0.9 copy-done.5
  5.0 0.0 copy-start.2
  5.0 63.6 %exchange.1 = (bf16[256,2048]{1,0:T(8,128)(2,1)S(1)}, bf16[8,256,256]{2,1,0:T(8,128)(2,1)S(1)}, bf16[8,256,256]{2,1,0:T(8,128)(2,1)S(1)}, s32[8,8,256]{2,1,0:T(8,128)S(1)}) custom-call(s32[64]{0:T(128)S(1)} %get-tuple-element.18.idx, s32[8,128]{1,0:T(8,128)S(1)} %select_reduce_fusion.wtab, bf16[16,64,128]{2,1,0:T(8,128)(2,1)S(1)} %bitcast_bitcast_fusion.kv, ...), custom_call_target="tpu_custom_call" | custom-call | tf_op jit(solution)/shard_map/exchange/pallas_call | solution.py:434
  68.7 0.0 copy-done.6
  68.7 0.0 copy-done.7
  68.7 0.0 copy-done
  68.7 0.0 copy-done.1
  68.7 0.0 copy-done.2
  68.7 38.2 %experts.1 = (bf16[2,1024,256]{2,1,0:T(8,128)(2,1)S(1)}, bf16[256,256]{1,0:T(8,128)(2,1)S(1)}, bf16[256,256]{1,0:T(8,128)(2,1)S(1)}) custom-call(bf16[256,2048]{1,0:T(8,128)(2,1)S(1)} %get-tuple-element.11.att, bf16[8,256,256]{2,1,0:T(8,128)(2,1)S(1)} %get-tuple-element.12.res, bf16[8,256,256]{2,1,0:T(8,128)(2,1)S(1)} %get-tuple-element.13.cot, ...), custom_call_target="tpu_custom_call" | custom-call | tf_op jit(solution)/shard_map/experts/pallas_call | solution.py:466
  107.0 1.1 %fusion.8 = (f32[1,1024,256]{2,1,0:T(8,128)}, f32[1,1024,256]{2,1,0:T(8,128)S(1)}) fusion(bf16[2,1024,256]{2,1,0:T(8,128)(2,1)S(1)} %get-tuple-element.17), kind=kLoop, calls=%fused_computation.41 | loop fusion | bytes 4194304 | tf_op jit(solution)/shard_map/slice | solution.py:538
  108.1 1.1 %copy.25 = f32[2,2,32,8,256]{4,3,1,2,0:T(8,128)} copy(f32[2,2,32,8,256]{4,3,2,1,0:T(8,128)S(1)} %bitcast.18) | data formatting | bytes 2097152 | tf_op jit(solution)/shard_map/reshape | solution.py:537
  109.2 0.7 copy.29
  109.9 0.7 copy.30
  (4 shorter events, 0.1 us)
Async XLA Ops:
  0.6 68.0 %copy-start.6 = (bf16[256,16]{0,1:T(8,128)(2,1)S(1)}, bf16[256,16]{0,1:T(8,128)(2,1)}, u32[]{:S(2)}) copy-start(bf16[256,16]{0,1:T(8,128)(2,1)} %param.19) | copy-start | bytes 24580
  0.7 1.4 %copy-start.9 = (s32[256,2]{0,1:T(2,128)S(1)}, s32[256,2]{0,1:T(2,128)}, u32[]{:S(2)}) copy-start(s32[256,2]{0,1:T(2,128)} %param.20) | copy-start | bytes 6148
  0.7 0.7 copy-start.8
  0.7 68.0 %copy-start.7 = (f32[256]{0:T(256)S(1)}, f32[256]{0:T(256)}, u32[]{:S(2)}) copy-start(f32[256]{0:T(256)} %param.18) | copy-start | bytes 3076
  0.7 2.5 %copy-start.3 = (bf16[32,2048]{1,0:T(8,128)(2,1)S(1)}, bf16[32,2048]{1,0:T(8,128)(2,1)}, u32[]{:S(2)}) copy-start(bf16[32,2048]{1,0:T(8,128)(2,1)} %q.1) | copy-start | bytes 393220
  2.0 66.6 %copy-start = (bf16[2,256,512]{2,1,0:T(8,128)(2,1)S(1)}, bf16[2,256,512]{2,1,0:T(8,128)(2,1)}, u32[]{:S(2)}) copy-start(bf16[2,256,512]{2,1,0:T(8,128)(2,1)} %w_in.1) | copy-start | bytes 1572868
  2.1 66.6 %copy-start.1 = (bf16[2,512,256]{2,1,0:T(8,128)(2,1)S(1)}, bf16[2,512,256]{2,1,0:T(8,128)(2,1)}, u32[]{:S(2)}) copy-start(bf16[2,512,256]{2,1,0:T(8,128)(2,1)} %w_out.1) | copy-start | bytes 1572868
  3.2 0.9 copy-start.4
  4.1 0.9 copy-start.5
  5.0 63.7 %copy-start.2 = (bf16[256,256]{1,0:T(8,128)(2,1)S(1)}, bf16[256,256]{1,0:T(8,128)(2,1)}, u32[]{:S(2)}) copy-start(bf16[256,256]{1,0:T(8,128)(2,1)} %out_proj.1) | copy-start | bytes 393220

commit v2 on v1

v2 whole, which is shorter than its diff:
```python
import math

import jax
import jax.numpy as jnp
from jax import lax
from jax.experimental import pallas as pl
from jax.experimental.pallas import tpu as pltpu
from jax.sharding import PartitionSpec as P

MESH = pl.DeviceIdType.MESH
BF = jnp.bfloat16
F32 = jnp.float32
HD = 32
NY, NX, NC, NZ = 8, 4, 2, 8
CAPE = 64

norm_eps = 1e-05
root_two_pi = 0.7978845608028654
cubic_term = 0.044715

TN = (((0,), (0,)), ((), ()))
NT = (((1,), (1,)), ((), ()))


def dot(a, b, dims=(((1,), (0,)), ((), ()))):
    return lax.dot_general(a, b, dims, preferred_element_type=F32)


def place():
    seq, z = lax.axis_index("seq"), lax.axis_index("expert")
    y = seq // (NX * NC)
    x = (seq // NC) % NX
    c = seq % NC
    return y, x, c, z


def device(y, x, c, z):
    return ((y * NX + x) * NC + c, z)


def send(src, dst, ssem, rsem, dev):
    copy = pltpu.make_async_remote_copy(
        src_ref=src, dst_ref=dst, send_sem=ssem, recv_sem=rsem, device_id=dev, device_id_type=MESH
    )
    copy.start()
    return copy


class Ring:
    def __init__(self, slots, ssem, rsem, up, down, far_up):
        self.slots, self.ssem, self.rsem = slots, ssem, rsem
        self.up, self.down, self.far_up = up, down, far_up
        self.copies = {}

    def go(self, frm, to, dev):
        self.copies[to] = send(self.slots(frm), self.slots(to), self.ssem(to), self.rsem(to), dev)

    def begin(self):
        self.go(0, 1, self.up)
        self.go(0, 7, self.down)

    def arrive(self, k):
        self.copies[k].wait_recv()
        if k < 3 or (k == 3 and self.far_up):
            self.go(k, k + 1, self.up)
        if k > 5 or (k == 5 and not self.far_up):
            self.go(k, k - 1, self.down)


def drain(ref, sem):
    pltpu.make_async_copy(ref, ref, sem).wait()


def layer_kernel(
    idx, wtab, ids, gain, router, k_hbm, v_hbm, q_hbm, res_hbm, cot_hbm, op_hbm, wi_hbm, wo_hbm,
    grads, layer_out, grad_stream,
    yb0, yb1, yb2, yb3, yb4, yb5, yb6, yb7,
    zr, zc, zi, wr, wsm, sb, rv, at, q, op, opp, w_in, w_out,
    before, sel, pk, rows, cots, gates, ga, gb, ret, rr, stream_own, inv_own,
    rc, t1, rx, t2, ry, full,
    cols, kv_l, m_l, y_s, y_r, z_s, z_r, w_s, w_r, x_s, x_r, a_s, a_r,
    r_s, r_r, c_s, c_r, gx_s, gx_r, gy_s, gy_r, hy_s, hy_r, hx_s, hx_r, hc_s, hc_r,
):
    y, x, c, z = place()
    row = [(dx, dc) for dx in range(NX) for dc in range(NC)]
    peers = [device(y, (x + dx) % NX, (c + dc) % NC, z) for dx, dc in row]
    partner = peers[1]
    x_dev = [device(y, (x + d) % NX, c, z) for d in range(NX)]
    y_dev = [device((y + d) % NY, x, c, z) for d in range(NY)]
    z_dev = [device(y, x, c, (z + NZ - d) % NZ) for d in range(NZ)]
    up_y, down_y = y_dev[1], y_dev[7]
    up_z, down_z = z_dev[7], z_dev[1]

    barrier = pltpu.get_barrier_semaphore()
    for dev in z_dev[1:] + y_dev[1:] + peers[1:]:
        pl.semaphore_signal(barrier, inc=1, device_id=dev, device_id_type=MESH)

    def fetch(src, dst, sem):
        copy = pltpu.make_async_copy(src, dst, sem)
        copy.start()
        return copy

    fetched = [fetch(k_hbm, cols.at[0], kv_l.at[0]), fetch(v_hbm, cols.at[1], kv_l.at[1])]
    got_res = fetch(res_hbm, zr.at[0], m_l.at[0])
    got_cot = fetch(cot_hbm, zc.at[0], m_l.at[1])
    later = [
        fetch(a, v, m_l.at[2 + i])
        for i, (a, v) in enumerate(((q_hbm, q), (op_hbm, op), (wi_hbm, w_in), (wo_hbm, w_out)))
    ]
    own_table = fetch(wtab, wsm.at[0], m_l.at[6])
    before[...] = jnp.where(
        lax.broadcasted_iota(jnp.int32, (256, 256), 0)
        < lax.broadcasted_iota(jnp.int32, (256, 256), 1),
        1.0,
        0.0,
    ).astype(BF)
    for i in range(2):
        fetched[i].wait()
        for n in range(16):
            yb0[n, i * HD : (i + 1) * HD, :] = cols[i, :, n * 128 : (n + 1) * 128]
    got_res.wait()
    got_cot.wait()
    pl.semaphore_wait(barrier, 21)

    ybs = [yb0, yb1, yb2, yb3, yb4, yb5, yb6, yb7]
    for r in range(1, 8):
        send(wtab, wr.at[r], w_s.at[0], w_r.at[0], peers[r])

    def y_ring(ch):
        return Ring(
            lambda k: ybs[k].at[pl.ds(ch * 4, 4)],
            lambda k: y_s.at[0],
            lambda k: y_r.at[ch, k - 1],
            up_y, down_y, ch < 2,
        )

    def z_ring(i, slots, far_up):
        return Ring(
            slots, lambda k: z_s.at[i // 2], lambda k: z_r.at[i, k - 1], up_z, down_z, far_up
        )

    def half(buf, h):
        return lambda k: buf.at[k, pl.ds(h * 128, 128)]

    ys = [y_ring(ch) for ch in range(4)]
    zs = [
        z_ring(0, half(zr, 0), True),
        z_ring(1, half(zr, 1), False),
        z_ring(2, half(zc, 0), True),
        z_ring(3, half(zc, 1), False),
    ]
    zids = z_ring(4, lambda k: ids if k == 0 else zi.at[k], True)
    zids.begin()
    for ch in range(4):
        ys[ch].begin()
        zs[ch].begin()

    drain(wr.at[pl.ds(1, 7)], w_r.at[0])
    rest = fetch(wr.at[pl.ds(1, 7)], wsm.at[pl.ds(1, 7)], m_l.at[7])
    own_table.wait()
    rest.wait()

    line = x * NC + c

    def pick(rel):
        source = ybs[(8 - rel) % 8]
        owner_row = (y + rel) % NY
        for r in (4, 5, 2, 3, 6, 7, 1, 0):
            dx, dc = row[r]
            asked = ((NX - dx) % NX) * NC + dc
            for s in range(2):
                block = wsm[asked, owner_row, line * 2 + s]
                if r == 0:
                    rv[rel * 2 + s] = source[block]
                else:
                    sb[rel, r - 1, s] = source[block]
            if r:
                send(
                    sb.at[rel, r - 1],
                    rv.at[pl.ds((r * 8 + rel) * 2, 2)],
                    x_s.at[0],
                    x_r.at[0],
                    peers[r],
                )

    expert_row = lax.broadcasted_iota(jnp.int32, (16, 256), 0)
    slot_row = lax.broadcasted_iota(jnp.int32, (CAPE, 256), 0).astype(F32)

    def one_row(table, e):
        return jnp.sum(jnp.where(expert_row == e, table, 0.0), 0, keepdims=True)

    def local(j):
        return 1 - c if j == 0 else c

    def prepare(k):
        listed = ids[...] if k == 0 else zi[k]
        hot = jnp.where(
            (listed[0:1] == expert_row) | (listed[1:2] == expert_row), 1.0, 0.0
        )
        rank = dot(hot.astype(BF), before[...])
        place_of = jnp.where(hot > 0.5, rank, -1.0)

        def selector(e):
            return jnp.where(slot_row == one_row(place_of, e), 1.0, 0.0).astype(BF)

        for j in range(2):
            picked = selector(2 * z + local(j))
            sel[j, k] = picked
            cots[j, k * CAPE : (k + 1) * CAPE, :] = dot(picked, zc[k]).astype(BF)
        if k == 0:
            for j in range(2):
                for d in range(NZ):
                    pk[j, d * CAPE : (d + 1) * CAPE, :] = selector(
                        2 * ((z + d) % NZ) + local(j)
                    )

    pick(0)
    for copy in later:
        copy.wait()
    for k in range(NZ):
        head = (z + NZ - k) % NZ
        opp[k * HD : (k + 1) * HD, :] = op[pl.ds(pl.multiple_of(head * HD, HD), HD), :]
    prepare(0)
    for k in (1, 2, 3):
        for ch in range(4):
            for slot in (k, 8 - k):
                ys[ch].arrive(slot)
                zs[ch].arrive(slot)
        for slot in (k, 8 - k):
            zids.arrive(slot)
            pick((8 - slot) % 8)
        for slot in (k, 8 - k):
            prepare(slot)
    for ring in ys:
        ring.arrive(4)
    pick(4)
    for ring in zs + [zids]:
        ring.arrive(4)
    prepare(4)
    drain(rv.at[pl.ds(16, 112)], x_r.at[0])

    rings = []

    def attend(ch):
        def block(i, carry):
            b = ch * 4 + i
            pairs = [rv[idx[b * 4 + j]] for j in range(4)]
            keys = jnp.concatenate([p[:HD] for p in pairs], 1)
            values = jnp.concatenate([p[HD:] for p in pairs], 1)
            queries = q[:, pl.ds(pl.multiple_of(b * 128, 128), 128)]
            scores = dot(keys, queries, TN) * (1.0 / math.sqrt(HD))
            weights = jnp.exp(scores - jnp.max(scores, 0, keepdims=True))
            total = jnp.sum(weights, 0, keepdims=True)
            out = dot(values, weights.astype(BF)) / total
            at[0, ch, :, pl.ds(pl.multiple_of(i * 128, 128), 128)] = out.astype(BF)
            return carry

        lax.fori_loop(0, 4, block, 0, unroll=True)
        ring = Ring(
            lambda k: at.at[k, ch],
            lambda k: a_s.at[0],
            lambda k: a_r.at[ch, k - 1],
            up_z, down_z, ch < 2,
        )
        ring.begin()
        rings.append(ring)

    def arrive(k, ch):
        rings[ch].arrive(k)
        if k < 4:
            rings[ch].arrive(8 - k)

    def home(ch):
        mixed = at[:, ch].reshape(256, 512)
        projected = dot(mixed, opp[...], TN)
        for i in range(2):
            k = (z + NZ - (2 * ch + i)) % NZ
            stream = (zr[k].astype(F32) + projected[i * 256 : (i + 1) * 256]).astype(BF)
            wide = stream.astype(F32)
            inv = lax.rsqrt(jnp.mean(wide * wide, -1, keepdims=True) + norm_eps)
            normed = (wide * inv * gain[...]).astype(BF)
            gate = jax.nn.sigmoid(dot(router[...], normed, NT))

            @pl.when(k == 0)
            def _():
                stream_own[...] = wide
                inv_own[...] = jnp.broadcast_to(inv, (256, 128))

            at_rows = pl.ds(pl.multiple_of(k * CAPE, CAPE), CAPE)
            for j in range(2):
                picked = sel[j, k]
                rows[j, at_rows, :] = dot(picked, normed).astype(BF)
                value = jnp.sum(
                    picked.astype(F32) * one_row(gate, 2 * z + local(j)), 1, keepdims=True
                )
                gates[j, at_rows, :] = jnp.broadcast_to(value, (CAPE, 128))

    attend(0)
    attend(1)
    attend(2)
    arrive(1, 0)
    attend(3)
    for k, ch in (
        (1, 1), (2, 0), (1, 2), (2, 1), (1, 3), (3, 0), (2, 2), (3, 1), (2, 3), (4, 0), (3, 2),
    ):
        arrive(k, ch)
    home(0)
    arrive(4, 1)
    arrive(3, 3)
    home(1)
    arrive(4, 2)
    home(2)
    arrive(4, 3)
    home(3)

    chains = range(2)

    def cross_x(i):
        pair[i].wait_recv()
        own = ga if i == 0 else gb
        t1[i] = (own[1].astype(F32) + rc[i].astype(F32)).astype(BF)
        for d in (2, 1, 3):
            to = (x + d) % NX
            send(
                t1.at[i, pl.ds(pl.multiple_of(to * 128, 128), 128)],
                rx.at[i, d], gx_s.at[i], gx_r.at[i], x_dev[d],
            )

    for j in range(2):
        e = local(j)
        inp, outp = w_in[e], w_out[e]
        x_rows = rows[j]
        gate = gates[j][:, 0:1]
        cot_rows = cots[j].astype(F32)
        scaled = (gate * cot_rows).astype(BF)
        pre = dot(x_rows, inp)
        grad_hidden = dot(scaled, outp, NT)
        square = pre * pre
        half_up = 0.5 + 0.5 * jnp.tanh(pre * (root_two_pi + root_two_pi * cubic_term * square))
        hidden = (pre * half_up).astype(BF)
        slope = half_up * (
            1.0
            + (1.0 - half_up) * pre * (2.0 * root_two_pi + 6.0 * root_two_pi * cubic_term * square)
        )
        grad_pre = (grad_hidden * slope).astype(BF)

        def weights_part():
            gb[j] = dot(hidden, scaled, TN).astype(BF)
            grad_in = dot(x_rows, grad_pre, TN).astype(BF)
            ga[j, 0:256, :] = grad_in[:, 0:256]
            ga[j, 256:512, :] = grad_in[:, 256:512]

        def rows_part():
            made = dot(hidden, outp)
            grad_rows = dot(grad_pre, inp, NT)
            grad_gate = jnp.sum(cot_rows * made, -1, keepdims=True)
            grad_logit = grad_gate * gate * (1.0 - gate)
            column = one_row(router[...].astype(F32), 2 * z + e)
            first = (gate * made).astype(BF)
            second = (grad_rows + grad_logit * column).astype(BF)
            for k in (4, 3, 5, 2, 6, 1, 7, 0):
                target = ret if k else rr
                target[j, k, :, 0:256] = first[k * CAPE : (k + 1) * CAPE]
                target[j, k, :, 256:512] = second[k * CAPE : (k + 1) * CAPE]
                if k:
                    send(ret.at[j, k], rr.at[j, k], r_s.at[j], r_r.at[j], z_dev[k])

        if j == 0:
            rows_part()
            weights_part()
            pair = [
                send(g.at[0], rc.at[i], c_s.at[i], c_r.at[i], partner)
                for i, g in enumerate((ga, gb))
            ]
        else:
            weights_part()
            for i in chains:
                cross_x(i)
            rows_part()

    for i in chains:
        total = t1[i, pl.ds(pl.multiple_of(x * 128, 128), 128), :].astype(F32)
        drain(rx.at[i, pl.ds(1, 3)], gx_r.at[i])
        for d in range(1, NX):
            total += rx[i, d].astype(F32)
        t2[i] = total.astype(BF)
        for d in (4, 3, 5, 2, 6, 1, 7):
            to = (y + d) % NY
            send(
                t2.at[i, pl.ds(pl.multiple_of(to * 16, 16), 16)],
                ry.at[i, d], gy_s.at[i], gy_r.at[i], y_dev[d],
            )

    def span(size):
        first = {16: x * 128 + y * 16, 128: x * 128, 512: 0}[size] + c * 512
        return pl.ds(pl.multiple_of(first, size), size)

    for i in chains:
        total = t2[i, pl.ds(pl.multiple_of(y * 16, 16), 16), :].astype(F32)
        drain(ry.at[i, pl.ds(1, 7)], gy_r.at[i])
        for d in range(1, NY):
            total += ry[i, d].astype(F32)
        full[i, span(16), :] = total.astype(BF)
        for d in (4, 3, 5, 2, 6, 1, 7):
            part = full.at[i, span(16)]
            send(part, part, hy_s.at[i], hy_r.at[i], y_dev[d])
    for i in chains:
        drain(ry.at[i, pl.ds(1, 7)], hy_r.at[i])
        for d in (2, 1, 3):
            part = full.at[i, span(128)]
            send(part, part, hx_s.at[i], hx_r.at[i], x_dev[d])

    def gathered(j):
        return dot(pk[j], rr[j].reshape(512, 512), TN)

    drain(rr.at[0, pl.ds(1, 7)], r_r.at[0])
    total = gathered(0)
    out_c = []
    for i in chains:
        drain(rx.at[i, pl.ds(1, 3)], hx_r.at[i])
        part = full.at[i, span(512)]
        out_c.append(send(part, part, hc_s.at[i], hc_r.at[i], partner))
    for copy in out_c:
        copy.wait_recv()
    kept = fetch(full, grads, m_l.at[8])

    drain(rr.at[1, pl.ds(1, 7)], r_r.at[1])
    total += gathered(1)
    wide, inv = stream_own[...], inv_own[...][:, 0:1]
    layer_out[...] = (wide + total[:, 0:256]).astype(BF)
    gained = total[:, 256:512] * gain[...]
    mean = jnp.mean(wide * gained, -1, keepdims=True)
    grad_stream[...] = (
        zc[0].astype(F32) + inv * gained - wide * (inv * inv * inv) * mean
    ).astype(BF)

    kept.wait()
    drain(wr.at[pl.ds(1, 7)], w_s.at[0])
    drain(rv.at[pl.ds(16, 112)], y_s.at[0])
    drain(zr.at[pl.ds(1, 7)], z_s.at[0])
    drain(zc.at[pl.ds(1, 7)], z_s.at[1])
    drain(zi.at[pl.ds(1, 7)], z_s.at[2])
    drain(sb, x_s.at[0])
    drain(at.at[pl.ds(1, 7)], a_s.at[0])
    for copy in pair + out_c:
        copy.wait_send()
    for i in chains:
        drain(ret.at[i, pl.ds(1, 7)], r_s.at[i])
        drain(rx.at[i, pl.ds(1, 3)], gx_s.at[i])
        drain(ry.at[i, pl.ds(1, 7)], gy_s.at[i])
        drain(ry.at[i, pl.ds(1, 7)], hy_s.at[i])
        drain(rx.at[i, pl.ds(1, 3)], hx_s.at[i])


VM = pl.BlockSpec(memory_space=pltpu.VMEM)
SM = pl.BlockSpec(memory_space=pltpu.SMEM)
HB = pl.BlockSpec(memory_space=pltpu.HBM)
DMA = pltpu.SemaphoreType.DMA


def layer(*args):
    def vm(*shape, dtype=BF):
        return pltpu.VMEM(shape, dtype)

    return pl.pallas_call(
        layer_kernel,
        name="layer",
        out_shape=(
            jax.ShapeDtypeStruct((2, 1024, 256), BF),
            jax.ShapeDtypeStruct((256, 256), BF),
            jax.ShapeDtypeStruct((256, 256), BF),
        ),
        in_specs=[SM] + [VM] * 4 + [HB] * 8,
        out_specs=(HB, VM, VM),
        scratch_shapes=[vm(16, 64, 128)] * 8
        + [
            vm(8, 256, 256), vm(8, 256, 256), vm(8, 2, 256, dtype=jnp.int32),
            vm(8, 8, 128, dtype=jnp.int32), pltpu.SMEM((8, 8, 128), jnp.int32),
            vm(8, 7, 2, 64, 128), vm(128, 64, 128), vm(8, 4, 32, 512),
            vm(32, 2048), vm(256, 256), vm(256, 256), vm(2, 256, 512), vm(2, 512, 256),
            vm(256, 256), vm(2, 8, CAPE, 256), vm(2, 512, 256),
            vm(2, 512, 256), vm(2, 512, 256), vm(2, 512, 128, dtype=F32),
            vm(2, 512, 256), vm(2, 512, 256), vm(2, 8, CAPE, 512), vm(2, 8, CAPE, 512),
            vm(256, 256, dtype=F32), vm(256, 128, dtype=F32),
            vm(2, 512, 256), vm(2, 512, 256), vm(2, 4, 128, 256),
            vm(2, 128, 256), vm(2, 8, 16, 256), vm(2, 1024, 256),
            vm(2, 32, 2048), DMA((2,)), DMA((9,)), DMA((1,)), DMA((4, 7)), DMA((3,)), DMA((5, 7)),
            DMA((1,)), DMA((1,)), DMA((1,)), DMA((1,)), DMA((1,)), DMA((4, 7)),
        ]
        + [DMA((2,))] * 14,
        compiler_params=pltpu.CompilerParams(
            collective_id=0, has_side_effects=True, vmem_limit_bytes=66_000_000
        ),
    )(*args)


def widen_kernel(
    grads, layer_in, grad_in, ga, gb, layer_out, grad_out, held, wide_a, wide_b, rows, i_s, o_s
):
    loads = [
        pltpu.make_async_copy(
            grads.at[i, pl.ds(e * 512, 512)], held.at[i, e], i_s.at[2 * i + e]
        )
        for i in range(2)
        for e in range(2)
    ]
    loads += [
        pltpu.make_async_copy(layer_in, rows.at[0], i_s.at[4]),
        pltpu.make_async_copy(grad_in, rows.at[1], i_s.at[5]),
    ]
    for load in loads:
        load.start()
    stores = []
    for n, load in enumerate(loads):
        load.wait()
        i, e = n // 2, n % 2
        if i == 0:
            wide_a[e, :, 0:256] = held[0, e, 0:256].astype(F32)
            wide_a[e, :, 256:512] = held[0, e, 256:512].astype(F32)
            pair = (wide_a.at[e], ga.at[e])
        elif i == 1:
            wide_b[e] = held[1, e].astype(F32)
            pair = (wide_b.at[e], gb.at[e])
        else:
            pair = (rows.at[e], (layer_out, grad_out)[e])
        store = pltpu.make_async_copy(pair[0], pair[1], o_s.at[n])
        store.start()
        stores.append(store)
    for store in stores:
        store.wait()


def widen(*args):
    return pl.pallas_call(
        widen_kernel,
        name="widen",
        out_shape=(
            jax.ShapeDtypeStruct((2, 256, 512), F32),
            jax.ShapeDtypeStruct((2, 512, 256), F32),
            jax.ShapeDtypeStruct((256, 256), BF),
            jax.ShapeDtypeStruct((256, 256), BF),
        ),
        in_specs=[HB] * 3,
        out_specs=(HB,) * 4,
        scratch_shapes=[
            pltpu.VMEM((2, 2, 512, 256), BF),
            pltpu.VMEM((2, 256, 512), F32),
            pltpu.VMEM((2, 512, 256), F32),
            pltpu.VMEM((2, 256, 256), BF),
            DMA((6,)),
            DMA((6,)),
        ],
        compiler_params=pltpu.CompilerParams(vmem_limit_bytes=66_000_000),
    )(*args)


def tables(block_list):
    y, x, c, _ = place()
    asked = block_list.reshape(-1)
    owner, inner = asked // 16, asked % 16
    entry = jnp.arange(64, dtype=jnp.int32)
    earlier = (owner[:, None] == owner[None, :]) & (entry[None, :] < entry[:, None])
    rank = jnp.sum(earlier.astype(jnp.int32), 1)
    owner_y, line = owner // (NX * NC), owner % (NX * NC)
    rows = jnp.arange(8, dtype=jnp.int32)[:, None, None]
    lanes = jnp.arange(128, dtype=jnp.int32)[None, :, None]
    hit = (owner_y[None, None, :] == rows) & ((line * 2 + rank)[None, None, :] == lanes)
    wanted = jnp.sum(jnp.where(hit, inner[None, None, :], 0), -1)
    supplier = (x - line // NC) % NX * NC + (c - line % NC) % NC
    index = (supplier * 8 + (owner_y - y) % NY) * 2 + rank
    return index, wanted


def shards(
    query_cols, key_cols, value_cols, block_list, residual, out_proj, norm_gain,
    router_weight, expert_ids, expert_in, expert_out, cotangent,
):
    index, wanted = tables(block_list)
    grads, layer_out, grad_stream = layer(
        index, wanted, expert_ids.T, norm_gain.reshape(1, 256), router_weight.T,
        key_cols, value_cols, query_cols, residual, cotangent, out_proj, expert_in, expert_out,
    )
    grad_in, grad_out, layer_out, grad_stream = widen(grads, layer_out, grad_stream)
    return layer_out, grad_stream, grad_in, grad_out


def solution(mesh):
    assert (mesh.shape["seq"], mesh.shape["expert"]) == (NY * NX * NC, NZ)
    return jax.shard_map(
        shards,
        mesh=mesh,
        in_specs=(
            P("expert", "seq"),
            P("expert", "seq"),
            P("expert", "seq"),
            P("seq", None),
            P(("seq", "expert"), None),
            P(),
            P(),
            P(),
            P(("seq", "expert"), None),
            P("expert", None, None),
            P("expert", None, None),
            P(("seq", "expert"), None),
        ),
        out_specs=(
            P(("seq", "expert"), None),
            P(("seq", "expert"), None),
            P("expert", None, None),
            P("expert", None, None),
        ),
        check_vma=False,
    )
```

time: 111 us -> 103 us (0.928)
  local copies, waits for them, and re-layouts: 6.21 us -> 0.84 us
  Pallas kernels: 102 us -> 99 us
    unnamed x23 -> x3, local copies, waits for them, and re-layouts: 3.86 us -> 0.76 us
    pallas_call x2, Pallas kernels: 102 us -> 99 us  [the longest x1 96.5 us: layer(): pl.pallas_call(layer_kernel, name='layer', out_shape=(jax.ShapeDtypeStruc...]
    slice x1 -> x0, local copies, waits for them, and re-layouts: 1.13 us -> none  [shards(): return (layer_out, grad_stream, grad_in, wide[1].reshape(2, 512, 256))]
    reshape x1 -> x0, local copies, waits for them, and re-layouts: 1.12 us -> none  [shards(): jnp.transpose(wide[0].reshape(2, 2, 256, 256), (0, 2, 1, 3))]
    transpose x1 -> x0, other arithmetic: 1.11 us -> none  [shards(): jnp.transpose(pairs, (1, 0, 2))]
where the time goes in v2:
time: 103 us; the launch traced here: 102 us
  Pallas kernels  99 us (96%)
  other arithmetic  1.57 us (2%)
    pallas_call x1, Pallas kernels, layer(): pl.pallas_call(layer_kernel, name='layer', out_shape=(jax.ShapeDtypeStruc...  96.5 us
    pallas_call x1, Pallas kernels, widen(): pl.pallas_call(widen_kernel, name='widen', out_shape=(jax.ShapeDtypeStruc...  2.48 us

profile of v2, /device:TPU:1, one launch (start us, length us, event | category | flops | bytes accessed | tf_op | source)
XLA Modules:
  0.0 102.3 jit_solution(7351237093915852710)
XLA Ops:
  0.7 0.0 copy-start
  0.7 0.7 copy-done
  1.4 0.1 copy.18
  1.4 0.1 reshape.204
  1.5 0.2 convert_reduce_fusion
  1.7 0.6 multiply_add_fusion.1
  2.3 0.1 iota_compare_fusion
  2.4 0.8 select_reduce_fusion.wtab
  3.1 96.5 %layer.1 = (bf16[2,1024,256]{2,1,0:T(8,128)(2,1)}, bf16[256,256]{1,0:T(8,128)(2,1)}, bf16[256,256]{1,0:T(8,128)(2,1)}) custom-call(s32[64]{0:T(128)} %get-tuple-element.18.idx, s32[8,128]{1,0:T(8,128)} %select_reduce_fusion.wtab, s32[2,256]{1,0:T(2,128)} %bitcast.4, f32[1,256]{1,0:T(1,128)} %bitcast.5, bf16[16,256]{1,0:T(8,128)(2,1)} %bitcast.3, ...), custom_call_target="tpu_custom_call" | custom-call | tf_op jit(solution)/shard_map/layer/pallas_call | solution.py:465
  99.6 2.5 %widen.1 = (f32[2,256,512]{2,1,0:T(8,128)}, f32[2,512,256]{2,1,0:T(8,128)}, bf16[256,256]{1,0:T(8,128)(2,1)}, bf16[256,256]{1,0:T(8,128)(2,1)}) custom-call(bf16[2,1024,256]{2,1,0:T(8,128)(2,1)} %get-tuple-element.11.grads, bf16[256,256]{1,0:T(8,128)(2,1)} %get-tuple-element.12.layer_in, bf16[256,256]{1,0:T(8,128)(2,1)} %get-tuple-element.13.grad_in), custom_call_target="tpu_custom_call" | custom-call | tf_op jit(solution)/shard_map/widen/pallas_call | solution.py:534
  (2 shorter events, 0.0 us)
Async XLA Ops:
  0.7 0.7 copy-start

commit v3 on v2

--- a/solution.py
+++ b/solution.py
@@ -76,7 +76,7 @@
     grads, layer_out, grad_stream,
     yb0, yb1, yb2, yb3, yb4, yb5, yb6, yb7,
     zr, zc, zi, wr, wsm, sb, rv, at, q, op, opp, w_in, w_out,
-    before, sel, pk, rows, cots, gates, ga, gb, ret, rr, stream_own, inv_own,
+    before, sel, pk, rows, cots, ga, gb, ret, rr,
     rc, t1, rx, t2, ry, full,
     cols, kv_l, m_l, y_s, y_r, z_s, z_r, w_s, w_r, x_s, x_r, a_s, a_r,
     r_s, r_r, c_s, c_r, gx_s, gx_r, gy_s, gy_r, hy_s, hy_r, hx_s, hx_r, hc_s, hc_r,
@@ -214,29 +214,44 @@
                         2 * ((z + d) % NZ) + local(j)
                     )
 
+    def arrive_y(k):
+        for ch in range(4):
+            for slot in (k, 8 - k):
+                ys[ch].arrive(slot)
+        for slot in (k, 8 - k):
+            pick((8 - slot) % 8)
+
+    def arrive_z(k):
+        for ch in range(4):
+            for slot in (k, 8 - k):
+                zs[ch].arrive(slot)
+        for slot in (k, 8 - k):
+            zids.arrive(slot)
+
     pick(0)
+    arrive_y(1)
+    arrive_z(1)
     for copy in later:
         copy.wait()
     for k in range(NZ):
         head = (z + NZ - k) % NZ
         opp[k * HD : (k + 1) * HD, :] = op[pl.ds(pl.multiple_of(head * HD, HD), HD), :]
-    prepare(0)
-    for k in (1, 2, 3):
-        for ch in range(4):
-            for slot in (k, 8 - k):
-                ys[ch].arrive(slot)
-                zs[ch].arrive(slot)
-        for slot in (k, 8 - k):
-            zids.arrive(slot)
-            pick((8 - slot) % 8)
-        for slot in (k, 8 - k):
-            prepare(slot)
+    for k in (0, 1, 7):
+        prepare(k)
+    arrive_y(2)
+    arrive_z(2)
+    for k in (2, 6):
+        prepare(k)
+    arrive_y(3)
     for ring in ys:
         ring.arrive(4)
     pick(4)
+    arrive_z(3)
     for ring in zs + [zids]:
         ring.arrive(4)
-    prepare(4)
+    for k in (3, 5, 4):
+        prepare(k)
+    drain(zr.at[pl.ds(1, 7)], z_s.at[0])
     drain(rv.at[pl.ds(16, 112)], x_r.at[0])
 
     rings = []
@@ -279,21 +294,10 @@
             wide = stream.astype(F32)
             inv = lax.rsqrt(jnp.mean(wide * wide, -1, keepdims=True) + norm_eps)
             normed = (wide * inv * gain[...]).astype(BF)
-            gate = jax.nn.sigmoid(dot(router[...], normed, NT))
-
-            @pl.when(k == 0)
-            def _():
-                stream_own[...] = wide
-                inv_own[...] = jnp.broadcast_to(inv, (256, 128))
-
+            zr[k] = stream
             at_rows = pl.ds(pl.multiple_of(k * CAPE, CAPE), CAPE)
             for j in range(2):
-                picked = sel[j, k]
-                rows[j, at_rows, :] = dot(picked, normed).astype(BF)
-                value = jnp.sum(
-                    picked.astype(F32) * one_row(gate, 2 * z + local(j)), 1, keepdims=True
-                )
-                gates[j, at_rows, :] = jnp.broadcast_to(value, (CAPE, 128))
+                rows[j, at_rows, :] = dot(sel[j, k], normed).astype(BF)
 
     attend(0)
     attend(1)
@@ -330,7 +334,11 @@
         e = local(j)
         inp, outp = w_in[e], w_out[e]
         x_rows = rows[j]
-        gate = gates[j][:, 0:1]
+        logits = dot(x_rows, router[...], NT)
+        lane = lax.broadcasted_iota(jnp.int32, (512, 16), 1)
+        gate = jax.nn.sigmoid(
+            jnp.sum(jnp.where(lane == 2 * z + e, logits, 0.0), 1, keepdims=True)
+        )
         cot_rows = cots[j].astype(F32)
         scaled = (gate * cot_rows).astype(BF)
         pre = dot(x_rows, inp)
@@ -426,7 +434,8 @@
 
     drain(rr.at[1, pl.ds(1, 7)], r_r.at[1])
     total += gathered(1)
-    wide, inv = stream_own[...], inv_own[...][:, 0:1]
+    wide = zr[0].astype(F32)
+    inv = lax.rsqrt(jnp.mean(wide * wide, -1, keepdims=True) + norm_eps)
     layer_out[...] = (wide + total[:, 0:256]).astype(BF)
     gained = total[:, 256:512] * gain[...]
     mean = jnp.mean(wide * gained, -1, keepdims=True)
@@ -437,7 +446,6 @@
     kept.wait()
     drain(wr.at[pl.ds(1, 7)], w_s.at[0])
     drain(rv.at[pl.ds(16, 112)], y_s.at[0])
-    drain(zr.at[pl.ds(1, 7)], z_s.at[0])
     drain(zc.at[pl.ds(1, 7)], z_s.at[1])
     drain(zi.at[pl.ds(1, 7)], z_s.at[2])
     drain(sb, x_s.at[0])
@@ -479,9 +487,8 @@
             vm(8, 7, 2, 64, 128), vm(128, 64, 128), vm(8, 4, 32, 512),
             vm(32, 2048), vm(256, 256), vm(256, 256), vm(2, 256, 512), vm(2, 512, 256),
             vm(256, 256), vm(2, 8, CAPE, 256), vm(2, 512, 256),
-            vm(2, 512, 256), vm(2, 512, 256), vm(2, 512, 128, dtype=F32),
+            vm(2, 512, 256), vm(2, 512, 256),
             vm(2, 512, 256), vm(2, 512, 256), vm(2, 8, CAPE, 512), vm(2, 8, CAPE, 512),
-            vm(256, 256, dtype=F32), vm(256, 128, dtype=F32),
             vm(2, 512, 256), vm(2, 512, 256), vm(2, 4, 128, 256),
             vm(2, 128, 256), vm(2, 8, 16, 256), vm(2, 1024, 256),
             vm(2, 32, 2048), DMA((2,)), DMA((9,)), DMA((1,)), DMA((4, 7)), DMA((3,)), DMA((5, 7)),

time: 103 us -> 102 us (level)
  no operation moved by 1% of the time
where the time goes in v3:
time: 102 us; the launch traced here: 101 us
  Pallas kernels  98.2 us (96%)
  other arithmetic  1.57 us (2%)
    pallas_call x1, Pallas kernels, layer(): pl.pallas_call(layer_kernel, name='layer', out_shape=(jax.ShapeDtypeStruc...  95.8 us
    pallas_call x1, Pallas kernels, widen(): pl.pallas_call(widen_kernel, name='widen', out_shape=(jax.ShapeDtypeStruc...  2.48 us

profile of v3, /device:TPU:1, one launch (start us, length us, event | category | flops | bytes accessed | tf_op | source)
XLA Modules:
  0.0 101.4 jit_solution(8013681490161626265)
XLA Ops:
  0.7 0.0 copy-start
  0.7 0.7 copy-done
  1.4 0.1 copy.18
  1.4 0.1 reshape.204
  1.5 0.2 convert_reduce_fusion
  1.7 0.6 multiply_add_fusion.1
  2.3 0.1 iota_compare_fusion
  2.4 0.8 select_reduce_fusion.wtab
  3.1 95.8 %layer.1 = (bf16[2,1024,256]{2,1,0:T(8,128)(2,1)}, bf16[256,256]{1,0:T(8,128)(2,1)}, bf16[256,256]{1,0:T(8,128)(2,1)}) custom-call(s32[64]{0:T(128)} %get-tuple-element.18.idx, s32[8,128]{1,0:T(8,128)} %select_reduce_fusion.wtab, s32[2,256]{1,0:T(2,128)} %bitcast.4, f32[1,256]{1,0:T(1,128)} %bitcast.5, bf16[16,256]{1,0:T(8,128)(2,1)} %bitcast.3, ...), custom_call_target="tpu_custom_call" | custom-call | tf_op jit(solution)/shard_map/layer/pallas_call | solution.py:473
  98.9 2.5 %widen.1 = (f32[2,256,512]{2,1,0:T(8,128)}, f32[2,512,256]{2,1,0:T(8,128)}, bf16[256,256]{1,0:T(8,128)(2,1)}, bf16[256,256]{1,0:T(8,128)(2,1)}) custom-call(bf16[2,1024,256]{2,1,0:T(8,128)(2,1)} %get-tuple-element.11.grads, bf16[256,256]{1,0:T(8,128)(2,1)} %get-tuple-element.12.layer_in, bf16[256,256]{1,0:T(8,128)(2,1)} %get-tuple-element.13.grad_in), custom_call_target="tpu_custom_call" | custom-call | tf_op jit(solution)/shard_map/widen/pallas_call | solution.py:541
  (2 shorter events, 0.0 us)
Async XLA Ops:
  0.7 0.7 copy-start
